TPU v7x, 32 devices: a whole 2x2x4 slice. The times are simulated.
32 devices in a mesh: tm: 4 (over y, x), space: 8 (over z, core).
Axes of the slice: x: 2, y: 2, z: 4, core: 2. Of those that a mesh axis runs over, the one named last changes fastest.
Arguments:
- queries: bfloat16 [4, 768, 3072], P('tm', 'space'), may hold values from -8 to 8
- key_rows: bfloat16 [4, 768, 3072], P('tm', 'space'), may hold values from -8 to 8
- value_rows: bfloat16 [4, 768, 3072], P('tm', 'space'), may hold values from -6 to 6
- noise_level: int32 [4], P('tm'), may hold values from 0 to 999
- decay_power: int32 [24], replicated, may hold values from 0 to 7
- head_gain: float32 [24, 128], replicated, may hold values from 0.1 to 1.9
Outputs:
- attended: bfloat16 [4, 768, 3072], P('tm', 'space')
All inputs are finite; a program needn't handle non-finite values.
Results may differ from a plain program's by a relative error of at most 0.0049.
Values may be sent and summed in bfloat16 or wider, within the bound.
A program may use at most 64 MiB of HBM per device.

v0:
```python
import jax
import jax.numpy as jnp
from jax import lax
from jax.sharding import PartitionSpec as P

LEVELS = 1000
HGROUPS = 8


epsilon = 1e-06


def carried_in(value, axis, join, neutral):
    count, mine = (lax.axis_size(axis), lax.axis_index(axis))
    pieces = jax.tree.map(lambda part: lax.all_gather(part, axis), value)
    so_far = jax.tree.map(
        lambda part, zero: jnp.full_like(part, 0) + jnp.asarray(zero, part.dtype), value, neutral
    )

    def lap(position, so_far):
        longer = join(so_far, jax.tree.map(lambda part: part[position], pieces))
        return jax.tree.map(lambda new, old: jnp.where(position < mine, new, old), longer, so_far)

    return lax.fori_loop(0, count - 1, lap, so_far)


def spread_items(block, quarters, heads_total, depth):
    part_rows = block.shape[0] // quarters
    shaped = block.reshape(quarters, part_rows, heads_total, depth).transpose(0, 2, 1, 3)
    return shaped.reshape(quarters * heads_total, part_rows, depth)


def copied_items(block, quarters, heads_total, depth):
    every = block.reshape(block.shape[0], heads_total, depth).transpose(1, 0, 2)
    copied = jnp.broadcast_to(every[None], (quarters,) + every.shape)
    return copied.reshape(quarters * heads_total, block.shape[0], depth)


def attend_head(bundle):
    query, key_item, value_item, state, gain_row = bundle
    factor = query.shape[1] ** (-0.5)
    scores = jnp.dot(query, key_item.T, preferred_element_type=jnp.float32) * factor
    row_top = jnp.max(scores, axis=1, keepdims=True)
    weights = jnp.exp(scores - row_top)
    row_total = jnp.sum(weights, axis=1, keepdims=True)
    numerator = jnp.dot(
        weights.astype(jnp.bfloat16), value_item, preferred_element_type=jnp.float32
    )
    carried = jnp.dot(query, state, preferred_element_type=jnp.float32) * factor
    mixed = numerator / row_total + carried
    normed = mixed * lax.rsqrt(jnp.mean(mixed * mixed, axis=1, keepdims=True) + epsilon) * gain_row
    return normed.astype(jnp.bfloat16)


def compose(earlier, later):
    return (earlier[0] * later[0], later[0][:, None, None] * earlier[1] + later[1])


def body(queries, key_rows, value_rows, noise_level, decay_power, head_gain):
    heads_total = decay_power.shape[0]
    depth = head_gain.shape[1]
    local_rows = queries.shape[1]
    quarters = lax.axis_size("space") // HGROUPS
    grouped = heads_total // HGROUPS
    query_items = spread_items(queries[0], quarters, heads_total, depth)
    keys_sent = copied_items(key_rows[0], quarters, heads_total, depth)
    values_sent = copied_items(value_rows[0], quarters, heads_total, depth)
    query_got, keys_got, values_got = (
        lax.all_to_all(query_items, "space", split_axis=0, concat_axis=1, tiled=True),
        lax.all_to_all(keys_sent, "space", split_axis=0, concat_axis=1, tiled=True),
        lax.all_to_all(values_sent, "space", split_axis=0, concat_axis=1, tiled=True),
    )
    key_count = keys_got.shape[1]
    fresh = (
        jnp.einsum("inh,ine->ihe", keys_got, values_got, preferred_element_type=jnp.float32)
        / key_count
    )
    group_index = lax.axis_index("space") % HGROUPS
    powers = lax.dynamic_slice_in_dim(decay_power, group_index * grouped, grouped).astype(
        jnp.float32
    )
    level_now = noise_level[0].astype(jnp.float32)
    block_count = lax.axis_size("tm")
    rate = jnp.exp2(-(powers * (0.25 + 1.75 * level_now / LEVELS)) / block_count)
    zeros_state = jnp.zeros_like(fresh)
    unused_rate, before = carried_in(
        (rate, fresh), "tm", compose, (jnp.ones_like(rate), zeros_state)
    )
    state = (rate[:, None, None] * before).astype(jnp.bfloat16)
    gain_rows = lax.dynamic_slice_in_dim(head_gain, group_index * grouped, grouped)
    outcome = lax.map(attend_head, (query_got, keys_got, values_got, state, gain_rows))
    returned = lax.all_to_all(outcome, "space", split_axis=1, concat_axis=0, tiled=True)
    part_rows = local_rows // quarters
    restored = returned.reshape(quarters, heads_total, part_rows, depth).transpose(0, 2, 1, 3)
    return restored.reshape(1, local_rows, heads_total * depth)


def solution(mesh):
    in_specs = (
        P("tm", "space", None),
        P("tm", "space", None),
        P("tm", "space", None),
        P("tm"),
        P(),
        P(),
    )
    out_specs = P("tm", "space", None)
    return jax.shard_map(body, mesh=mesh, in_specs=in_specs, out_specs=out_specs, check_vma=False)
```

profile of v0, /device:TPU:0, one launch (start us, length us, event | category | flops | bytes accessed | tf_op | source)
XLA Modules:
  0.0 99.5 jit_solution(8693053812802755996)
XLA Ops:
  0.0 0.0 copy-start
  0.0 0.0 copy-start.1
  0.0 1.2 %copy.38 = bf16[12,8,24,128]{3,2,1,0:T(8,128)(2,1)S(1)} copy(bf16[12,8,24,128]{3,1,2,0:T(8,128)(2,1)} %bitcast.111) | data formatting | bytes 1179648
  1.2 0.9 copy.26
  2.1 0.0 copy-start.4
  2.1 0.0 copy-start.3
  2.2 0.0 copy-start.2
  2.2 6.5 %all-to-all-start.1 = ((bf16[24,96,128]{2,1,0:T(8,128)(2,1)}), bf16[24,96,128]{2,1,0:T(8,128)(2,1)S(1)}, u32[]{:S(2)}, u32[]{:S(2)}) async-start(bf16[24,96,128]{2,1,0:T(8,128)(2,1)} %copy.26), calls=%async_computation.1 | async-start | bytes 1179648 | tf_op jit(solution)/shard_map/all_to_all | solution.py:70
  8.6 0.0 copy-done.1
  8.6 0.1 copy.39
  8.8 0.9 copy.28
  9.7 15.7 %all-to-all-done.1 = bf16[24,96,128]{2,1,0:T(8,128)(2,1)S(1)} async-done(((bf16[24,96,128]{2,1,0:T(8,128)(2,1)}), bf16[24,96,128]{2,1,0:T(8,128)(2,1)S(1)}, u32[]{:S(2)}, u32[]{:S(2)}) %all-to-all-start.1) | async-done | bytes 589856 | tf_op jit(solution)/shard_map/all_to_all | solution.py:70
  25.4 3.5 %all-to-all-start.2 = ((bf16[24,96,128]{2,1,0:T(8,128)(2,1)}), bf16[24,96,128]{2,1,0:T(8,128)(2,1)S(1)}, u32[]{:S(2)}, u32[]{:S(2)}) async-start(bf16[24,96,128]{2,1,0:T(8,128)(2,1)} %copy.28), calls=%async_computation.2 | async-start | bytes 1179648 | tf_op jit(solution)/shard_map/all_to_all | solution.py:71
  29.6 0.0 copy-done.4
  29.6 0.6 dynamic-slice
  30.9 0.0 copy-done.3
  30.9 0.2 fusion.25
  31.0 9.9 %all-reduce = f32[12]{0:T(128)S(1)} all-reduce(f32[12]{0:T(128)S(1)} %get-tuple-element.187), channel_id=2, replica_groups=mesh['tm'=4,'space'=8] {'tm'}, use_global_device_ids=true, to_apply=%add | all-reduce | flops 12 | bytes 96
  40.9 0.1 reshape.30
  41.0 0.0 copy-done.2
  41.0 0.1 copy.37
  41.1 0.1 bitcast_bitcast_fusion
  41.2 0.9 copy.24
  42.1 0.0 copy-done
  42.2 3.4 %all-to-all-done.2 = bf16[24,96,128]{2,1,0:T(8,128)(2,1)S(1)} async-done(((bf16[24,96,128]{2,1,0:T(8,128)(2,1)}), bf16[24,96,128]{2,1,0:T(8,128)(2,1)S(1)}, u32[]{:S(2)}, u32[]{:S(2)}) %all-to-all-start.2) | async-done | bytes 589856 | tf_op jit(solution)/shard_map/all_to_all | solution.py:71
  45.6 3.5 %all-to-all-start = ((bf16[24,96,128]{2,1,0:T(8,128)(2,1)}), bf16[24,96,128]{2,1,0:T(8,128)(2,1)S(1)}, u32[]{:S(2)}, u32[]{:S(2)}) async-start(bf16[24,96,128]{2,1,0:T(8,128)(2,1)} %copy.24), calls=%async_computation | async-start | bytes 1179648 | tf_op jit(solution)/shard_map/all_to_all | solution.py:69
  49.2 0.4 convolution_multiply_fusion.1
  49.5 12.5 %all-gather.1 = f32[12,128,128]{2,1,0:T(8,128)S(1)} all-gather(f32[3,128,128]{2,1,0:T(8,128)S(1)} %convolution_multiply_fusion.1), channel_id=3, replica_groups=mesh['tm'=4,'space'=8] {'tm'}, dimensions={0}, use_global_device_ids=true | all-gather | bytes 983040 | tf_op jit(solution)/shard_map/all_gather | solution.py:15
  62.1 0.4 while.25
  62.1 0.1 fusion.39
  62.2 0.1 fusion.39
  62.4 0.1 fusion.39
  62.5 3.3 %all-to-all-done = bf16[24,96,128]{2,1,0:T(8,128)(2,1)S(1)} async-done(((bf16[24,96,128]{2,1,0:T(8,128)(2,1)}), bf16[24,96,128]{2,1,0:T(8,128)(2,1)S(1)}, u32[]{:S(2)}, u32[]{:S(2)}) %all-to-all-start) | async-done | bytes 589856 | tf_op jit(solution)/shard_map/all_to_all | solution.py:69
  65.8 0.1 multiply_convert_fusion.1
  65.9 7.7 %while.24 = (s32[]{:T(128)}, bf16[3,768,128]{1,2,0:T(8,128)(2,1)}, bf16[3,768,128]{2,1,0:T(8,128)(2,1)S(1)}, bf16[3,768,128]{2,1,0:T(8,128)(2,1)S(1)}, bf16[3,76...) while((s32[]{:T(128)}, bf16[3,768,128]{1,2,0:T(8,128)(2,1)}, ...), condition=%wide.region_6.7_spmd, body=%wide.region_2.6_spmd.sunk | while | flops 332659968 | bytes 9700445 | solution.py:91
  65.9 0.5 multiply_reduce_fusion.4
  66.4 0.4 fusion.36
  66.8 0.2 convolution_multiply_fusion.3
  67.1 0.6 multiply_reduce_fusion.5
  67.7 0.8 fusion.38
  68.5 0.5 multiply_reduce_fusion.4
  69.0 0.4 fusion.36
  69.4 0.3 convolution_multiply_fusion.3
  69.7 0.6 multiply_reduce_fusion.5
  70.3 0.8 fusion.38
  71.0 0.5 multiply_reduce_fusion.4
  71.5 0.4 fusion.36
  71.9 0.3 convolution_multiply_fusion.3
  72.2 0.6 multiply_reduce_fusion.5
  72.8 0.8 fusion.38
  73.6 1.5 %copy.31 = bf16[3,768,128]{2,0,1:T(4,128)(2,1)S(1)} copy(bf16[3,768,128]{1,2,0:T(8,128)(2,1)} %get-tuple-element.137) | data formatting | bytes 1179648 | tf_op jit(solution)/shard_map/while | solution.py:91
  75.1 23.4 %all_to_all.69 = bf16[3,768,128]{2,0,1:T(4,128)(2,1)S(1)} all-to-all(bf16[3,768,128]{2,0,1:T(4,128)(2,1)S(1)} %copy.31), channel_id=1, replica_groups=mesh['tm'=4,'space'=8] {'space'}, dimensions={1} | all-to-all | bytes 1179648 | tf_op jit(solution)/shard_map/all_to_all | solution.py:92
  98.4 0.1 copy.32
  98.6 1.0 copy.41
  (17 shorter events, 0.3 us)
Async XLA Ops:
  0.0 42.1 %copy-start = (f32[24,128]{1,0:T(8,128)S(1)}, f32[24,128]{1,0:T(8,128)}, u32[]{:S(2)}) copy-start(f32[24,128]{1,0:T(8,128)} %param.15) | copy-start | bytes 36868
  0.0 8.6 %copy-start.1 = (bf16[1,96,3072]{2,1,0:T(8,128)(2,1)S(1)}, bf16[1,96,3072]{2,1,0:T(8,128)(2,1)}, u32[]{:S(2)}) copy-start(bf16[1,96,3072]{2,1,0:T(8,128)(2,1)} %param.12) | copy-start | bytes 1769476
  2.1 27.4 %copy-start.4 = (u32[32]{0:T(128)S(1)}, u32[32]{0:T(128)}, u32[]{:S(2)}) copy-start(u32[32]{0:T(128)} %constant.102) | copy-start | bytes 388
  2.1 28.7 %copy-start.3 = (s32[24]{0:T(128)S(1)}, s32[24]{0:T(128)}, u32[]{:S(2)}) copy-start(s32[24]{0:T(128)} %param.14) | copy-start | bytes 292
  2.2 38.9 %copy-start.2 = (bf16[1,96,3072]{2,1,0:T(8,128)(2,1)S(1)}, bf16[1,96,3072]{2,1,0:T(8,128)(2,1)}, u32[]{:S(2)}) copy-start(bf16[1,96,3072]{2,1,0:T(8,128)(2,1)} %param.10) | copy-start | bytes 1769476
  2.2 23.2 %all-to-all-start.1 = ((bf16[24,96,128]{2,1,0:T(8,128)(2,1)}), bf16[24,96,128]{2,1,0:T(8,128)(2,1)S(1)}, u32[]{:S(2)}, u32[]{:S(2)}) async-start(bf16[24,96,128]{2,1,0:T(8,128)(2,1)} %copy.26), calls=%async_computation.1 | async-start | bytes 1179648 | tf_op jit(solution)/shard_map/all_to_all | solution.py:70
  25.4 20.2 %all-to-all-start.2 = ((bf16[24,96,128]{2,1,0:T(8,128)(2,1)}), bf16[24,96,128]{2,1,0:T(8,128)(2,1)S(1)}, u32[]{:S(2)}, u32[]{:S(2)}) async-start(bf16[24,96,128]{2,1,0:T(8,128)(2,1)} %copy.28), calls=%async_computation.2 | async-start | bytes 1179648 | tf_op jit(solution)/shard_map/all_to_all | solution.py:71
  45.6 20.2 %all-to-all-start = ((bf16[24,96,128]{2,1,0:T(8,128)(2,1)}), bf16[24,96,128]{2,1,0:T(8,128)(2,1)S(1)}, u32[]{:S(2)}, u32[]{:S(2)}) async-start(bf16[24,96,128]{2,1,0:T(8,128)(2,1)} %copy.24), calls=%async_computation | async-start | bytes 1179648 | tf_op jit(solution)/shard_map/all_to_all | solution.py:69
where the time goes:
time: 100 us; the launch traced here: 99.5 us
  blocking collectives  45.8 us (46%)
  waiting for transfers between devices  22.4 us (22%)
  starting transfers between devices  13.6 us (14%)
  local copies, waits for them, and re-layouts  7.68 us (8%)
  matrix products  4.3 us (4%)
  other arithmetic  4.18 us (4%)
  between operations  1.48 us (1%)
    all_to_all x1, blocking collectives, body(): lax.all_to_all(outcome, 'space', split_axis=1, concat_axis=0, tiled=True)  23.4 us
    all_to_all x1, waiting for transfers between devices, body(): lax.all_to_all(keys_sent, 'space', split_axis=0, concat_axis=1, tiled=True)  15.7 us
    all_gather x1, blocking collectives, carried_in(): pieces = jax.tree.map(lambda part: lax.all_gather(part, axis), value)  12.5 us
    unnamed x1, blocking collectives  9.88 us
    all_to_all x1, starting transfers between devices, body(): lax.all_to_all(keys_sent, 'space', split_axis=0, concat_axis=1, tiled=True)  6.49 us
    all_to_all x1, starting transfers between devices, body(): lax.all_to_all(values_sent, 'space', split_axis=0, concat_axis=1, tiled=T...  3.54 us
    all_to_all x1, starting transfers between devices, body(): lax.all_to_all(query_items, 'space', split_axis=0, concat_axis=1, tiled=T...  3.54 us
    all_to_all x1, waiting for transfers between devices, body(): lax.all_to_all(values_sent, 'space', split_axis=0, concat_axis=1, tiled=T...  3.4 us
  transfers between devices with their start and end apart: 3, of which 3 were waited for; matrix products, arithmetic and copies ran while one was open for 4% of the time, Pallas kernels for 0%

commit v1 on v0

--- a/solution.py
+++ b/solution.py
@@ -1,6 +1,10 @@
+import functools
+
 import jax
 import jax.numpy as jnp
 from jax import lax
+from jax.experimental import pallas as pl
+from jax.experimental.pallas import tpu as pltpu
 from jax.sharding import PartitionSpec as P
 
 LEVELS = 1000
@@ -54,6 +58,178 @@
 
 def compose(earlier, later):
     return (earlier[0] * later[0], later[0][:, None, None] * earlier[1] + later[1])
+
+
+MESH = pl.DeviceIdType.MESH
+
+
+def partner(me, flips, count):
+    other, digit = me, 1
+    while digit < count:
+        if flips & digit:
+            other = other + digit * (1 - 2 * ((me // digit) % 2))
+        digit *= 2
+    return other
+
+
+def fused_kernel(
+    count, blocks, q_ref, k_ref, v_ref, noise_ref, power_ref, gain_ref, out_ref,
+    q_all, k_all, v_all, outcome, fresh_mine, fresh_got,
+    in_send, in_recv, out_send, out_recv, fresh_send, fresh_recv,
+):
+    rows = q_ref.shape[0]
+    depth = gain_ref.shape[1]
+    grouped = q_all.shape[0]
+    total_rows = count * rows
+    factor = depth ** (-0.5)
+    me, now = lax.axis_index("space"), lax.axis_index("tm")
+    peers = [partner(me, flips, count) for flips in range(count)]
+    order = list(range(count // 2, count)) + list(range(count // 2 - 1, 0, -1))
+
+    barrier = pltpu.get_barrier_semaphore()
+    for flips in range(1, count):
+        pl.semaphore_signal(barrier, inc=1, device_id={"space": peers[flips]}, device_id_type=MESH)
+    for step in range(1, blocks):
+        pl.semaphore_signal(
+            barrier, inc=1, device_id={"tm": lax.rem(now + step, blocks)}, device_id_type=MESH
+        )
+    pl.semaphore_wait(barrier, count - 1 + blocks - 1)
+
+    def lanes(head):
+        return pl.ds(pl.multiple_of(head * depth, depth), depth)
+
+    def part(device):
+        return pl.ds(pl.multiple_of(device * rows, rows), rows)
+
+    arrays = ((k_ref, k_all), (v_ref, v_all), (q_ref, q_all))
+    for slot in range(grouped):
+        for which, (source, target) in enumerate(arrays):
+            for flips in order:
+                pltpu.make_async_remote_copy(
+                    src_ref=source.at[:, lanes(peers[flips] * grouped + slot)],
+                    dst_ref=target.at[slot, part(me)],
+                    send_sem=in_send.at[slot, which],
+                    recv_sem=in_recv.at[slot, which],
+                    device_id={"space": peers[flips]},
+                    device_id_type=MESH,
+                ).start()
+            pltpu.make_async_copy(
+                source.at[:, lanes(me * grouped + slot)],
+                target.at[slot, part(me)],
+                in_recv.at[slot, which],
+            ).start()
+
+    def arrived(slot, which):
+        whole = arrays[which][1].at[slot]
+        pltpu.make_async_copy(whole, whole, in_recv.at[slot, which]).wait()
+
+    level = jnp.full((8, depth), noise_ref[0], jnp.int32).astype(jnp.float32)
+    for slot in range(grouped):
+        head = me * grouped + slot
+        power = jnp.full((8, depth), power_ref[head], jnp.int32).astype(jnp.float32)
+        rate = jnp.exp2(-(power * (0.25 + 1.75 * level / LEVELS)) / blocks)
+        arrived(slot, 0)
+        arrived(slot, 1)
+        fresh = lax.dot_general(
+            k_all[slot], v_all[slot], (((0,), (0,)), ((), ())), preferred_element_type=jnp.float32
+        )
+        fresh_mine[slot, 0:depth, :] = fresh / total_rows
+        fresh_mine[slot, depth : depth + 8, :] = rate
+        for step in range(1, blocks):
+            pltpu.make_async_remote_copy(
+                src_ref=fresh_mine.at[slot],
+                dst_ref=fresh_got.at[slot, step - 1],
+                send_sem=fresh_send.at[slot],
+                recv_sem=fresh_recv.at[slot],
+                device_id={"tm": lax.rem(now + step, blocks)},
+                device_id_type=MESH,
+            ).start()
+        arrived(slot, 2)
+        landed = fresh_got.at[slot]
+        pltpu.make_async_copy(landed, landed, fresh_recv.at[slot]).wait()
+        carried = jnp.zeros((depth, depth), jnp.float32)
+        for step in range(blocks - 1, 0, -1):
+            longer = (
+                fresh_got[slot, step - 1, depth : depth + 1, :] * carried
+                + fresh_got[slot, step - 1, 0:depth, :]
+            )
+            carried = jnp.where(now - step >= 0, longer, carried)
+        state = (rate[0:1, :] * carried).astype(jnp.bfloat16)
+        gain_row = gain_ref[pl.ds(head, 1), :]
+
+        def attend(device):
+            query = q_all[slot, part(device), :]
+            scores = lax.dot_general(
+                query, k_all[slot], (((1,), (1,)), ((), ())), preferred_element_type=jnp.float32
+            ) * factor
+            weights = jnp.exp(scores - jnp.max(scores, axis=1, keepdims=True))
+            row_total = jnp.sum(weights, axis=1, keepdims=True)
+            numerator = jnp.dot(
+                weights.astype(jnp.bfloat16), v_all[slot], preferred_element_type=jnp.float32
+            )
+            before = jnp.dot(query, state, preferred_element_type=jnp.float32) * factor
+            mixed = numerator / row_total + before
+            scale = lax.rsqrt(jnp.mean(mixed * mixed, axis=1, keepdims=True) + epsilon)
+            outcome[slot, part(device), :] = (mixed * scale * gain_row).astype(jnp.bfloat16)
+
+        for flips in order:
+            attend(peers[flips])
+            pltpu.make_async_remote_copy(
+                src_ref=outcome.at[slot, part(peers[flips])],
+                dst_ref=out_ref.at[:, lanes(head)],
+                send_sem=out_send.at[slot],
+                recv_sem=out_recv.at[0],
+                device_id={"space": peers[flips]},
+                device_id_type=MESH,
+            ).start()
+        attend(me)
+        pltpu.make_async_copy(
+            outcome.at[slot, part(me)], out_ref.at[:, lanes(head)], out_recv.at[0]
+        ).start()
+
+    for slot in range(grouped):
+        for which in range(len(arrays)):
+            sent = arrays[which][1].at[slot, pl.ds(0, total_rows - rows)]
+            pltpu.make_async_copy(sent, sent, in_send.at[slot, which]).wait()
+        landed = fresh_got.at[slot]
+        pltpu.make_async_copy(landed, landed, fresh_send.at[slot]).wait()
+        returned = outcome.at[slot, pl.ds(0, total_rows - rows)]
+        pltpu.make_async_copy(returned, returned, out_send.at[slot]).wait()
+    pltpu.make_async_copy(out_ref, out_ref, out_recv.at[0]).wait()
+
+
+def fused(queries, key_rows, value_rows, noise_level, decay_power, head_gain):
+    count, blocks = lax.axis_size("space"), lax.axis_size("tm")
+    rows, width = queries.shape[1:]
+    heads_total, depth = head_gain.shape
+    grouped = heads_total // count
+    gathered = pltpu.VMEM((grouped, count * rows, depth), jnp.bfloat16)
+    dma = pltpu.SemaphoreType.DMA
+    out = pl.pallas_call(
+        functools.partial(fused_kernel, count, blocks),
+        out_shape=jax.ShapeDtypeStruct((rows, width), jnp.bfloat16),
+        in_specs=[pl.BlockSpec(memory_space=pl.ANY)] * 3
+        + [pl.BlockSpec(memory_space=pltpu.SMEM)] * 2
+        + [pl.BlockSpec(memory_space=pltpu.VMEM)],
+        out_specs=pl.BlockSpec(memory_space=pl.ANY),
+        scratch_shapes=[
+            gathered,
+            gathered,
+            gathered,
+            gathered,
+            pltpu.VMEM((grouped, depth + 8, depth), jnp.float32),
+            pltpu.VMEM((grouped, blocks - 1, depth + 8, depth), jnp.float32),
+            dma((grouped, 3)),
+            dma((grouped, 3)),
+            dma((grouped,)),
+            dma((1,)),
+            dma((grouped,)),
+            dma((grouped,)),
+        ],
+        compiler_params=pltpu.CompilerParams(collective_id=0, has_side_effects=True),
+        name="heads_exchange",
+    )(queries[0], key_rows[0], value_rows[0], noise_level, decay_power, head_gain)
+    return out[None]
 
 
 def body(queries, key_rows, value_rows, noise_level, decay_power, head_gain):
@@ -105,4 +281,5 @@
         P(),
     )
     out_specs = P("tm", "space", None)
-    return jax.shard_map(body, mesh=mesh, in_specs=in_specs, out_specs=out_specs, check_vma=False)
+    step = fused if mesh.shape["space"] == HGROUPS else body
+    return jax.shard_map(step, mesh=mesh, in_specs=in_specs, out_specs=out_specs, check_vma=False)

time: 100 us -> 64.4 us (0.64)
  Pallas kernels: 0 us -> 61.6 us
  blocking collectives: 45.8 us -> 0 us
  waiting for transfers between devices: 22.4 us -> 0 us
  starting transfers between devices: 13.6 us -> 0 us
  local copies, waits for them, and re-layouts: 7.68 us -> 1.92 us
  matrix products: 4.3 us -> 0 us
  other arithmetic: 4.18 us -> 0 us
    pallas_call x0 -> x1, Pallas kernels: none -> 61.6 us  [fused(): pl.pallas_call(functools.partial(fused_kernel, count, blocks), out_shape=...]
    all_to_all x1 -> x0, blocking collectives: 23.4 us -> none  [body(): lax.all_to_all(outcome, 'space', split_axis=1, concat_axis=0, tiled=True)]
    all_to_all x3 -> x0, waiting for transfers between devices: 22.4 us -> none  [the longest x1 15.7 us: body(): lax.all_to_all(keys_sent, 'space', split_axis=0, concat_axis=1, tiled=True)]
    all_to_all x3 -> x0, starting transfers between devices: 13.6 us -> none  [the longest x1 6.49 us: body(): lax.all_to_all(keys_sent, 'space', split_axis=0, concat_axis=1, tiled=True)]
    all_gather x1 -> x0, blocking collectives: 12.5 us -> none  [carried_in(): pieces = jax.tree.map(lambda part: lax.all_gather(part, axis), value)]
    unnamed x1 -> x0, blocking collectives: 9.88 us -> none
    dot_general x10 -> x0, matrix products: 4.3 us -> none  [the longest x3 1.75 us: attend_head(): jnp.dot(weights.astype(jnp.bfloat16), value_item, preferred_element_type=...]
    dynamic_update_slice x3 -> x0, other arithmetic: 2.32 us -> none  [body(): lax.map(attend_head, (query_got, keys_got, values_got, state, gain_rows))]
  transfers between devices with their start and end apart: 3 -> 0, of which waited for: 3 -> 0; matrix products, arithmetic and copies ran while one was open for 4% -> 0% of each run, Pallas kernels for 0% -> 0%
where the time goes in v1:
time: 64.4 us; the launch traced here: 64.2 us
  Pallas kernels  61.6 us (96%)
  local copies, waits for them, and re-layouts  1.92 us (3%)
  between operations  0.66 us (1%)
    pallas_call x1, Pallas kernels, fused(): pl.pallas_call(functools.partial(fused_kernel, count, blocks), out_shape=...  61.6 us
    unnamed x1, local copies, waits for them, and re-layouts  1.92 us

profile of v1, /device:TPU:0, one launch (start us, length us, event | category | flops | bytes accessed | tf_op | source)
XLA Modules:
  0.0 64.2 jit_solution(2565555710490124138)
XLA Ops:
  0.7 61.6 %heads_exchange.1 = bf16[96,3072]{1,0:T(8,128)(2,1)} custom-call(bf16[96,3072]{1,0:T(8,128)(2,1)} %bitcast.5, bf16[96,3072]{1,0:T(8,128)(2,1)} %bitcast.6, bf16[96,3072]{1,0:T(8,128)(2,1)} %bitcast.7, s32[1]{0:T(128)S(6)} %copy.8.noise_ref, s32[24]{0:T(128)} %power_ref.1, f32[24,128]{1,0:T(8,128)} %gain_ref.1), custom_call_target="tpu_custom_call" | custom-call | tf_op jit(solution)/shard_map/heads_exchange/pallas_call | solution.py:208
  62.3 1.9 %copy.9 = bf16[1,96,3072]{2,1,0:T(8,128)(2,1)} copy(bf16[1,96,3072]{2,1,0:T(8,128)(2,1)} %bitcast.4) | data formatting | bytes 1179648

commit v2 on v1

--- a/solution.py
+++ b/solution.py
@@ -9,6 +9,7 @@
 
 LEVELS = 1000
 HGROUPS = 8
+VMEM_GRANT = 32 * 2**20
 
 
 epsilon = 1e-06
@@ -73,7 +74,8 @@
 
 
 def fused_kernel(
-    count, blocks, q_ref, k_ref, v_ref, noise_ref, power_ref, gain_ref, out_ref,
+    count, blocks, q_ref, k_ref, v_ref, noise_ref, power_hbm, gain_hbm, out_ref,
+    power_ref, gain_ref, small_done,
     q_all, k_all, v_all, outcome, fresh_mine, fresh_got,
     in_send, in_recv, out_send, out_recv, fresh_send, fresh_recv,
 ):
@@ -84,7 +86,16 @@
     factor = depth ** (-0.5)
     me, now = lax.axis_index("space"), lax.axis_index("tm")
     peers = [partner(me, flips, count) for flips in range(count)]
-    order = list(range(count // 2, count)) + list(range(count // 2 - 1, 0, -1))
+    order = list(range(1, count))
+
+    small = [
+        pltpu.make_async_copy(held, here, small_done.at[index])
+        for index, (held, here) in enumerate(
+            ((power_hbm, power_ref), (gain_hbm, gain_ref))
+        )
+    ]
+    for copy in small:
+        copy.start()
 
     barrier = pltpu.get_barrier_semaphore()
     for flips in range(1, count):
@@ -102,9 +113,9 @@
         return pl.ds(pl.multiple_of(device * rows, rows), rows)
 
     arrays = ((k_ref, k_all), (v_ref, v_all), (q_ref, q_all))
-    for slot in range(grouped):
+    def send_inputs(slot, others):
         for which, (source, target) in enumerate(arrays):
-            for flips in order:
+            for flips in others:
                 pltpu.make_async_remote_copy(
                     src_ref=source.at[:, lanes(peers[flips] * grouped + slot)],
                     dst_ref=target.at[slot, part(me)],
@@ -113,6 +124,14 @@
                     device_id={"space": peers[flips]},
                     device_id_type=MESH,
                 ).start()
+
+    near, far = order[: count // 2 - 1], order[count // 2 - 1 :]
+    for slot in range(grouped):
+        send_inputs(slot, near)
+    for slot in range(grouped):
+        send_inputs(slot, far)
+    for slot in range(grouped):
+        for which, (source, target) in enumerate(arrays):
             pltpu.make_async_copy(
                 source.at[:, lanes(me * grouped + slot)],
                 target.at[slot, part(me)],
@@ -123,12 +142,28 @@
         whole = arrays[which][1].at[slot]
         pltpu.make_async_copy(whole, whole, in_recv.at[slot, which]).wait()
 
+    def give_back(slot, flips):
+        pltpu.make_async_remote_copy(
+            src_ref=outcome.at[slot, part(peers[flips])],
+            dst_ref=out_ref.at[:, lanes(me * grouped + slot)],
+            send_sem=out_send.at[slot],
+            recv_sem=out_recv.at[0],
+            device_id={"space": peers[flips]},
+            device_id_type=MESH,
+        ).start()
+
+    for copy in small:
+        copy.wait()
     level = jnp.full((8, depth), noise_ref[0], jnp.int32).astype(jnp.float32)
     for slot in range(grouped):
         head = me * grouped + slot
         power = jnp.full((8, depth), power_ref[head], jnp.int32).astype(jnp.float32)
         rate = jnp.exp2(-(power * (0.25 + 1.75 * level / LEVELS)) / blocks)
         arrived(slot, 0)
+        if slot == grouped - 1:
+            for earlier in range(slot):
+                for flips in order:
+                    give_back(earlier, flips)
         arrived(slot, 1)
         fresh = lax.dot_general(
             k_all[slot], v_all[slot], (((0,), (0,)), ((), ())), preferred_element_type=jnp.float32
@@ -174,14 +209,8 @@
 
         for flips in order:
             attend(peers[flips])
-            pltpu.make_async_remote_copy(
-                src_ref=outcome.at[slot, part(peers[flips])],
-                dst_ref=out_ref.at[:, lanes(head)],
-                send_sem=out_send.at[slot],
-                recv_sem=out_recv.at[0],
-                device_id={"space": peers[flips]},
-                device_id_type=MESH,
-            ).start()
+            if slot == grouped - 1:
+                give_back(slot, flips)
         attend(me)
         pltpu.make_async_copy(
             outcome.at[slot, part(me)], out_ref.at[:, lanes(head)], out_recv.at[0]
@@ -203,16 +232,23 @@
     rows, width = queries.shape[1:]
     heads_total, depth = head_gain.shape
     grouped = heads_total // count
+    held = [
+        pltpu.with_memory_space_constraint(operand, pltpu.HBM)
+        for operand in (queries[0], key_rows[0], value_rows[0], decay_power, head_gain)
+    ]
     gathered = pltpu.VMEM((grouped, count * rows, depth), jnp.bfloat16)
     dma = pltpu.SemaphoreType.DMA
     out = pl.pallas_call(
         functools.partial(fused_kernel, count, blocks),
         out_shape=jax.ShapeDtypeStruct((rows, width), jnp.bfloat16),
         in_specs=[pl.BlockSpec(memory_space=pl.ANY)] * 3
-        + [pl.BlockSpec(memory_space=pltpu.SMEM)] * 2
-        + [pl.BlockSpec(memory_space=pltpu.VMEM)],
+        + [pl.BlockSpec(memory_space=pltpu.SMEM)]
+        + [pl.BlockSpec(memory_space=pl.ANY)] * 2,
         out_specs=pl.BlockSpec(memory_space=pl.ANY),
         scratch_shapes=[
+            pltpu.SMEM(decay_power.shape, jnp.int32),
+            pltpu.VMEM(head_gain.shape, jnp.float32),
+            dma((2,)),
             gathered,
             gathered,
             gathered,
@@ -226,9 +262,9 @@
             dma((grouped,)),
             dma((grouped,)),
         ],
-        compiler_params=pltpu.CompilerParams(collective_id=0, has_side_effects=True),
+        compiler_params=pltpu.CompilerParams(collective_id=0, has_side_effects=True, vmem_limit_bytes=VMEM_GRANT),
         name="heads_exchange",
-    )(queries[0], key_rows[0], value_rows[0], noise_level, decay_power, head_gain)
+    )(*held[:3], noise_level, *held[3:])
     return out[None]
 
 

time: 64.4 us -> 59.2 us (0.919)
  Pallas kernels: 61.6 us -> 57.6 us
  local copies, waits for them, and re-layouts: 1.92 us -> 0.82 us
    pallas_call x1, Pallas kernels: 61.6 us -> 57.6 us  [fused(): pl.pallas_call(functools.partial(fused_kernel, count, blocks), out_shape=...]
    unnamed x1, local copies, waits for them, and re-layouts: 1.92 us -> 0.82 us
where the time goes in v2:
time: 59.2 us; the launch traced here: 59.1 us
  Pallas kernels  57.6 us (97%)
  local copies, waits for them, and re-layouts  0.82 us (1%)
  between operations  0.66 us (1%)
    pallas_call x1, Pallas kernels, fused(): pl.pallas_call(functools.partial(fused_kernel, count, blocks), out_shape=...  57.6 us

profile of v2, /device:TPU:0, one launch (start us, length us, event | category | flops | bytes accessed | tf_op | source)
XLA Modules:
  0.0 59.1 jit_solution(15215571441518904998)
XLA Ops:
  0.7 57.6 %heads_exchange.1 = bf16[96,3072]{1,0:T(8,128)(2,1)S(1)} custom-call(bf16[96,3072]{1,0:T(8,128)(2,1)} %bitcast.5, bf16[96,3072]{1,0:T(8,128)(2,1)} %bitcast.6, bf16[96,3072]{1,0:T(8,128)(2,1)} %bitcast.7, s32[1]{0:T(128)S(6)} %copy.8.noise_ref, s32[24]{0:T(128)} %power_hbm.1, f32[24,128]{1,0:T(8,128)} %gain_hbm.1), custom_call_target="tpu_custom_call" | custom-call | tf_op jit(solution)/shard_map/heads_exchange/pallas_call | solution.py:241
  58.3 0.8 %copy.9 = bf16[1,96,3072]{2,1,0:T(8,128)(2,1)} copy(bf16[1,96,3072]{2,1,0:T(8,128)(2,1)S(1)} %bitcast.4) | data formatting | bytes 1179648

commit v3 on v2

--- a/solution.py
+++ b/solution.py
@@ -160,10 +160,6 @@
         power = jnp.full((8, depth), power_ref[head], jnp.int32).astype(jnp.float32)
         rate = jnp.exp2(-(power * (0.25 + 1.75 * level / LEVELS)) / blocks)
         arrived(slot, 0)
-        if slot == grouped - 1:
-            for earlier in range(slot):
-                for flips in order:
-                    give_back(earlier, flips)
         arrived(slot, 1)
         fresh = lax.dot_general(
             k_all[slot], v_all[slot], (((0,), (0,)), ((), ())), preferred_element_type=jnp.float32
@@ -212,6 +208,10 @@
             if slot == grouped - 1:
                 give_back(slot, flips)
         attend(me)
+        if slot == grouped - 2:
+            for earlier in range(slot + 1):
+                for flips in far + near:
+                    give_back(earlier, flips)
         pltpu.make_async_copy(
             outcome.at[slot, part(me)], out_ref.at[:, lanes(head)], out_recv.at[0]
         ).start()

time: 59.2 us -> 58.5 us (0.988)
  Pallas kernels: 57.6 us -> 56.9 us
    pallas_call x1, Pallas kernels: 57.6 us -> 56.9 us  [fused(): pl.pallas_call(functools.partial(fused_kernel, count, blocks), out_shape=...]
where the time goes in v3:
time: 58.5 us; the launch traced here: 58.3 us
  Pallas kernels  56.9 us (97%)
  local copies, waits for them, and re-layouts  0.82 us (1%)
  between operations  0.66 us (1%)
    pallas_call x1, Pallas kernels, fused(): pl.pallas_call(functools.partial(fused_kernel, count, blocks), out_shape=...  56.9 us

profile of v3, /device:TPU:0, one launch (start us, length us, event | category | flops | bytes accessed | tf_op | source)
XLA Modules:
  0.0 58.3 jit_solution(463769505596454388)
XLA Ops:
  0.7 56.9 %heads_exchange.1 = bf16[96,3072]{1,0:T(8,128)(2,1)S(1)} custom-call(bf16[96,3072]{1,0:T(8,128)(2,1)} %bitcast.5, bf16[96,3072]{1,0:T(8,128)(2,1)} %bitcast.6, bf16[96,3072]{1,0:T(8,128)(2,1)} %bitcast.7, s32[1]{0:T(128)S(6)} %copy.8.noise_ref, s32[24]{0:T(128)} %power_hbm.1, f32[24,128]{1,0:T(8,128)} %gain_hbm.1), custom_call_target="tpu_custom_call" | custom-call | tf_op jit(solution)/shard_map/heads_exchange/pallas_call | solution.py:241
  57.5 0.8 %copy.9 = bf16[1,96,3072]{2,1,0:T(8,128)(2,1)} copy(bf16[1,96,3072]{2,1,0:T(8,128)(2,1)S(1)} %bitcast.4) | data formatting | bytes 1179648

commit v4 on v3

--- a/solution.py
+++ b/solution.py
@@ -113,8 +113,9 @@
         return pl.ds(pl.multiple_of(device * rows, rows), rows)
 
     arrays = ((k_ref, k_all), (v_ref, v_all), (q_ref, q_all))
-    def send_inputs(slot, others):
-        for which, (source, target) in enumerate(arrays):
+    def send_inputs(slot, others, chosen=range(len(arrays))):
+        for which in chosen:
+            source, target = arrays[which]
             for flips in others:
                 pltpu.make_async_remote_copy(
                     src_ref=source.at[:, lanes(peers[flips] * grouped + slot)],
@@ -126,10 +127,11 @@
                 ).start()
 
     near, far = order[: count // 2 - 1], order[count // 2 - 1 :]
+    send_inputs(0, far, (0,))
     for slot in range(grouped):
         send_inputs(slot, near)
     for slot in range(grouped):
-        send_inputs(slot, far)
+        send_inputs(slot, far, range(1 if slot == 0 else 0, len(arrays)))
     for slot in range(grouped):
         for which, (source, target) in enumerate(arrays):
             pltpu.make_async_copy(

time: 58.5 us -> 58.6 us (level)
  no operation moved by 1% of the time
where the time goes in v4:
time: 58.6 us; the launch traced here: 58.5 us
  Pallas kernels  57 us (97%)
  local copies, waits for them, and re-layouts  0.82 us (1%)
  between operations  0.66 us (1%)
    pallas_call x1, Pallas kernels, fused(): pl.pallas_call(functools.partial(fused_kernel, count, blocks), out_shape=...  57 us

profile of v4, /device:TPU:0, one launch (start us, length us, event | category | flops | bytes accessed | tf_op | source)
XLA Modules:
  0.0 58.5 jit_solution(14980911781811046324)
XLA Ops:
  0.7 57.0 %heads_exchange.1 = bf16[96,3072]{1,0:T(8,128)(2,1)S(1)} custom-call(bf16[96,3072]{1,0:T(8,128)(2,1)} %bitcast.5, bf16[96,3072]{1,0:T(8,128)(2,1)} %bitcast.6, bf16[96,3072]{1,0:T(8,128)(2,1)} %bitcast.7, s32[1]{0:T(128)S(6)} %copy.8.noise_ref, s32[24]{0:T(128)} %power_hbm.1, f32[24,128]{1,0:T(8,128)} %gain_hbm.1), custom_call_target="tpu_custom_call" | custom-call | tf_op jit(solution)/shard_map/heads_exchange/pallas_call | solution.py:243
  57.6 0.8 %copy.9 = bf16[1,96,3072]{2,1,0:T(8,128)(2,1)} copy(bf16[1,96,3072]{2,1,0:T(8,128)(2,1)S(1)} %bitcast.4) | data formatting | bytes 1179648
